TPU v7x, 512 devices: a whole 4x4x16 slice. The times are simulated.
512 devices in a mesh: grp: 32 (over y, x, core), shard: 16 (over z).
Axes of the slice: x: 4, y: 4, z: 16, core: 2. Of those that a mesh axis runs over, the one named last changes fastest.
Arguments:
- grads: bfloat16 [2, 32, 16, 768, 768], P(None, 'grp', 'shard')
- vec_grads: bfloat16 [2, 32, 16, 8, 768], P(None, 'grp', 'shard'), may hold values from -0.5 to 0.5
- weight: float32 [768, 768], P('shard'), may hold values from -0.21875 to 0.21875
- basis: float32 [768, 256], replicated, may hold values from -0.21875 to 0.21875
- moment: float32 [768, 256], P('shard'), may hold values from -4 to 4
- second: float32 [768, 256], P('shard'), may hold values from 0.01 to 1
- vectors: float32 [8, 768], P(None, 'shard'), may hold values from -6 to 6
- vec_moment: float32 [8, 768], P(None, 'shard'), may hold values from -1.5 to 1.5
- vec_second: float32 [8, 768], P(None, 'shard'), may hold values from 0.001 to 0.1
Outputs:
- new_weight: float32 [768, 768], P('shard')
- update: bfloat16 [768, 768], P('shard')
- new_moment: float32 [768, 256], P('shard')
- new_second: float32 [768, 256], P('shard')
- new_basis: float32 [768, 256], replicated
- new_vectors: float32 [8, 768], P(None, 'shard')
- new_vec_moment: float32 [8, 768], P(None, 'shard')
- new_vec_second: float32 [8, 768], P(None, 'shard')
All inputs are finite; a program needn't handle non-finite values.
Results may differ from a plain program's by a relative error of at most 0.001.
Values sent between devices are 32-bit elements; how exact they have to be, the bound alone decides.
A program may use at most 64 MiB of HBM per device.

v0:
```python
import jax
import jax.numpy as jnp
from jax import lax
from jax.sharding import PartitionSpec as P

NS_STEPS = 5
STEP = 100
HIGH = lax.Precision.HIGHEST


def matmul(left, right):
    return jnp.dot(left, right, precision=HIGH, preferred_element_type=jnp.float32)


def per_device(grads, vec_grads, weight, basis, moment, second, vectors, vec_moment, vec_second):
    shards = lax.axis_size("shard")
    width = grads.shape[-1]
    rows = weight.shape[0]
    cols = vectors.shape[1]
    me = lax.axis_index("shard")
    summed = grads[0, 0, 0].astype(jnp.float32) + grads[1, 0, 0].astype(jnp.float32)
    vec_local = vec_grads[0, 0, 0].astype(jnp.float32) + vec_grads[1, 0, 0].astype(jnp.float32)
    packed = jnp.concatenate([summed, vec_local], axis=0)
    packed = lax.psum(packed, ("grp", "shard"))
    total = packed[:width]
    vec_total = packed[width:]
    projected_all = matmul(total, basis)
    subspace = lax.dot_general(
        total,
        projected_all,
        (((0,), (0,)), ((), ())),
        precision=HIGH,
        preferred_element_type=jnp.float32,
    )
    squares = jnp.sum(total * total) + jnp.sum(vec_total * vec_total)
    iterate = subspace / jnp.sqrt(jnp.sum(subspace * subspace) + 1e-06)
    for step in range(NS_STEPS):
        gram = matmul(iterate.T, iterate)
        iterate = 1.5 * iterate - 0.5 * matmul(iterate, gram)
    factor = 1.0 / jnp.maximum(jnp.sqrt(squares / (width * width + vec_total.size)), 1.0)
    projected = lax.dynamic_slice_in_dim(projected_all, me * rows, rows, axis=0)
    vec_sum = lax.dynamic_slice_in_dim(vec_total, me * cols, cols, axis=1)
    first_fix = 1.0 - 0.9**STEP
    second_fix = 1.0 - 0.999**STEP
    grad_low = factor * projected
    new_moment = 0.9 * moment + 0.1 * grad_low
    new_second = 0.999 * second + 0.001 * grad_low * grad_low
    normalized = new_moment / first_fix / (jnp.sqrt(new_second / second_fix) + 1e-08)
    full = lax.dot_general(
        normalized,
        basis,
        (((1,), (1,)), ((), ())),
        precision=HIGH,
        preferred_element_type=jnp.float32,
    )
    new_weight = weight - 0.001 * (0.25 * full + 0.01 * weight)
    vec_grad = factor * vec_sum
    new_vec_moment = 0.9 * vec_moment + 0.1 * vec_grad
    new_vec_second = 0.999 * vec_second + 0.001 * vec_grad * vec_grad
    vec_step = new_vec_moment / first_fix / (jnp.sqrt(new_vec_second / second_fix) + 1e-08)
    new_vectors = vectors - 0.001 * (vec_step + 0.01 * vectors)
    return (
        new_weight,
        full.astype(jnp.bfloat16),
        new_moment,
        new_second,
        iterate,
        new_vectors,
        new_vec_moment,
        new_vec_second,
    )


def solution(mesh):
    return jax.shard_map(
        per_device,
        mesh=mesh,
        in_specs=(
            P(None, "grp", "shard", None, None),
            P(None, "grp", "shard", None, None),
            P("shard", None),
            P(),
            P("shard", None),
            P("shard", None),
            P(None, "shard"),
            P(None, "shard"),
            P(None, "shard"),
        ),
        out_specs=(
            P("shard", None),
            P("shard", None),
            P("shard", None),
            P("shard", None),
            P(),
            P(None, "shard"),
            P(None, "shard"),
            P(None, "shard"),
        ),
        check_vma=False,
    )
```

profile of v0, /device:TPU:1, one launch (start us, length us, event | category | flops | bytes accessed | tf_op | source)
XLA Modules:
  0.0 534.5 jit_solution(420021904912794236)
XLA Ops:
  7.2 0.0 copy-start
  7.2 0.0 all-reduce.2.cloned.1.call-start
  7.2 0.8 add_bitcast_fusion.1
  8.0 1.9 add_bitcast_fusion
  9.9 1.6 pad_maximum_fusion
  11.5 0.0 all-reduce.2.cloned.1.call-update
  11.5 485.5 %all-reduce.2.cloned.1.call-done = f32[776,768]{1,0:T(8,128)} async-done(((f32[776,768]{1,0:T(8,128)}), f32[776,768]{1,0:T(8,128)}) %all-reduce.2.cloned.1.call-update) | async-done | bytes 2383888 | tf_op jit(solution)/shard_map/psum | solution.py:24
  497.0 3.0 multiply_reduce_fusion
  500.0 1.3 fusion.25
  502.7 2.0 fusion.2
  504.8 5.3 multiply_reduce_fusion.1
  510.9 2.9 fusion.9
  513.8 0.8 fusion.8
  514.6 1.4 fusion.27
  516.0 0.8 fusion.7
  516.8 1.6 fusion.28
  518.4 0.8 fusion.6
  519.2 1.4 fusion.29
  520.7 0.8 fusion.5
  521.5 1.4 fusion.30
  522.9 1.7 fusion.4
  524.6 0.8 multiply_add_fusion
  525.5 1.5 fusion.26
  527.0 0.7 multiply_subtract_fusion.1
  (23 shorter events, 0.1 us)
Async XLA Ops:
  7.2 495.5 %copy-start = (f32[768,256]{1,0:T(8,128)S(1)}, f32[768,256]{1,0:T(8,128)}, u32[]{:S(2)}) copy-start(f32[768,256]{1,0:T(8,128)} %param.12) | copy-start | bytes 2359300
  7.2 489.8 %all-reduce.2.cloned.1.call-start = ((), (), s32[]{:S(2)}) async-start(), calls=%async_computation | async-start | bytes 4767744 | tf_op jit(solution)/shard_map/psum | solution.py:24
  497.0 5.8 %copy-start.1 = (f32[776,768]{1,0:T(8,128)S(1)}, f32[776,768]{1,0:T(8,128)}, u32[]{:S(2)}) copy-start(f32[776,768]{1,0:T(8,128)} %all-reduce.2.cloned.1.call-done) | copy-start | bytes 7151620
  504.7 5.3 %copy-start.2 = (f32[768,256]{1,0:T(8,128)}, f32[768,256]{1,0:T(8,128)S(1)}, u32[]{:S(2)}) copy-start(f32[768,256]{1,0:T(8,128)S(1)} %fusion.2) | copy-start | bytes 2359300
  510.1 3.7 copy-start.3
  520.6 4.0 copy-start.7
  520.6 4.0 copy-start.8
  521.4 4.0 copy-start.6
  521.5 5.5 %copy-start.9 = (f32[8,48]{1,0:T(8,128)S(1)}, f32[8,48]{1,0:T(8,128)}, u32[]{:S(2)}) copy-start(f32[8,48]{1,0:T(8,128)} %param.15) | copy-start | bytes 4612
  521.5 5.5 %copy-start.10 = (f32[8,48]{1,0:T(8,128)S(1)}, f32[8,48]{1,0:T(8,128)}, u32[]{:S(2)}) copy-start(f32[8,48]{1,0:T(8,128)} %param.16) | copy-start | bytes 4612
  521.5 5.5 %copy-start.11 = (f32[8,48]{1,0:T(8,128)S(1)}, f32[8,48]{1,0:T(8,128)}, u32[]{:S(2)}) copy-start(f32[8,48]{1,0:T(8,128)} %param.17) | copy-start | bytes 4612
  525.4 2.3 copy-start.4
  525.4 2.3 copy-start.5
Sparse Core Ops, SparseCore 0:
  13.4 483.5 all-reduce.1
where the time goes:
time: 535 us
  waiting for transfers between devices  485 us (91%)
  matrix products  22.4 us (4%)
  between operations  16.4 us (3%)
  other arithmetic  10.1 us (2%)
    psum x1, waiting for transfers between devices, per_device(): packed = lax.psum(packed, ('grp', 'shard'))  485 us
    dot_general x11, matrix products, matmul(): jnp.dot(left, right, precision=HIGH, preferred_element_type=jnp.float32)  15.6 us
  transfers between devices with their start and end apart: 1, of which 1 were waited for; matrix products, arithmetic and copies ran while one was open for 0% of the time, Pallas kernels for 0%

commit v1 on v0

--- a/solution.py
+++ b/solution.py
@@ -21,7 +21,7 @@
     summed = grads[0, 0, 0].astype(jnp.float32) + grads[1, 0, 0].astype(jnp.float32)
     vec_local = vec_grads[0, 0, 0].astype(jnp.float32) + vec_grads[1, 0, 0].astype(jnp.float32)
     packed = jnp.concatenate([summed, vec_local], axis=0)
-    packed = lax.psum(packed, ("grp", "shard"))
+    packed = lax.psum(lax.psum(packed, "grp"), "shard")
     total = packed[:width]
     vec_total = packed[width:]
     projected_all = matmul(total, basis)

time: 535 us -> 342 us (0.64)
  the two profiles are of different devices: /device:TPU:1 before, /device:TPU:2 now
where the time goes in v1:
time: 342 us; the launch traced here: 341 us
  waiting for transfers between devices  292 us (85%)
  matrix products  22.4 us (7%)
  between operations  16.4 us (5%)
  other arithmetic  10.1 us (3%)
    psum x2, waiting for transfers between devices, per_device(): packed = lax.psum(lax.psum(packed, 'grp'), 'shard')  292 us
    dot_general x11, matrix products, matmul(): jnp.dot(left, right, precision=HIGH, preferred_element_type=jnp.float32)  15.6 us
  transfers between devices with their start and end apart: 2, of which 2 were waited for; matrix products, arithmetic and copies ran while one was open for 0% of the time, Pallas kernels for 0%

profile of v1, /device:TPU:2, one launch (start us, length us, event | category | flops | bytes accessed | tf_op | source)
XLA Modules:
  0.0 341.3 jit_solution(7855629543243052)
XLA Ops:
  7.2 0.0 all-reduce.3.cloned.1.call-start
  7.2 0.8 add_bitcast_fusion.1
  8.0 1.9 add_bitcast_fusion
  9.9 1.6 pad_maximum_fusion
  11.5 0.0 all-reduce.5.cloned.1.call-start
  11.5 142.9 %all-reduce.3.cloned.1.call-done = f32[776,768]{1,0:T(8,128)} async-done(((f32[776,768]{1,0:T(8,128)}), f32[776,768]{1,0:T(8,128)}) %all-reduce.3.cloned.1.call-update) | async-done | bytes 2383888 | tf_op jit(solution)/shard_map/psum | solution.py:24
  154.5 149.2 %all-reduce.5.cloned.1.call-done = f32[776,768]{1,0:T(8,128)} async-done(((f32[776,768]{1,0:T(8,128)}), f32[776,768]{1,0:T(8,128)}) %all-reduce.5.cloned.1.call-update) | async-done | bytes 2383888 | tf_op jit(solution)/shard_map/psum | solution.py:24
  303.7 3.0 multiply_reduce_fusion
  306.7 1.3 fusion.25
  309.5 2.0 fusion.2
  311.5 5.3 %multiply_reduce_fusion.1 = (f32[]{:T(128)}, f32[768,256]{1,0:T(8,128)}) fusion(f32[768,256]{1,0:T(8,128)S(1)} %fusion.2, f32[776,768]{1,0:T(8,128)S(1)} %copy-done.1), kind=kOutput, calls=%fused_computation.17 | convolution fusion | flops 1812332544 | bytes 3932164 | tf_op jit(solution)/shard_map/dot_general | solution.py:28
  317.6 2.9 fusion.9
  320.5 0.8 fusion.8
  321.3 1.4 fusion.27
  322.7 0.8 fusion.7
  323.5 1.6 fusion.28
  325.1 0.8 fusion.6
  325.9 1.4 fusion.29
  327.4 0.8 fusion.5
  328.2 1.4 fusion.30
  329.7 1.7 fusion.4
  331.3 0.8 multiply_add_fusion
  332.2 1.5 fusion.26
  333.7 0.7 multiply_subtract_fusion.1
  (26 shorter events, 0.1 us)
Async XLA Ops:
  7.2 302.3 %copy-start = (f32[768,256]{1,0:T(8,128)S(1)}, f32[768,256]{1,0:T(8,128)}, u32[]{:S(2)}) copy-start(f32[768,256]{1,0:T(8,128)} %param.12) | copy-start | bytes 2359300
  7.2 147.2 %all-reduce.3.cloned.1.call-start = ((), (), s32[]{:S(2)}) async-start(), calls=%async_computation | async-start | bytes 4767744 | tf_op jit(solution)/shard_map/psum | solution.py:24
  11.5 292.2 %all-reduce.5.cloned.1.call-start = ((), (), s32[]{:S(2)}) async-start(), calls=%async_computation.1 | async-start | bytes 4767744 | tf_op jit(solution)/shard_map/psum | solution.py:24
  303.7 5.8 %copy-start.1 = (f32[776,768]{1,0:T(8,128)S(1)}, f32[776,768]{1,0:T(8,128)}, u32[]{:S(2)}) copy-start(f32[776,768]{1,0:T(8,128)} %all-reduce.5.cloned.1.call-done) | copy-start | bytes 7151620
  311.5 5.3 %copy-start.2 = (f32[768,256]{1,0:T(8,128)}, f32[768,256]{1,0:T(8,128)S(1)}, u32[]{:S(2)}) copy-start(f32[768,256]{1,0:T(8,128)S(1)} %fusion.2) | copy-start | bytes 2359300
  316.8 3.7 %copy-start.3 = (f32[768,256]{1,0:T(8,128)S(1)}, f32[768,256]{1,0:T(8,128)}, u32[]{:S(2)}) copy-start(f32[768,256]{1,0:T(8,128)} %get-tuple-element.18) | copy-start | bytes 2359300
  327.4 4.0 %copy-start.7 = (f32[48,256]{1,0:T(8,128)S(1)}, f32[48,256]{1,0:T(8,128)}, u32[]{:S(2)}) copy-start(f32[48,256]{1,0:T(8,128)} %param.13) | copy-start | bytes 147460
  327.4 4.0 %copy-start.8 = (f32[48,256]{1,0:T(8,128)S(1)}, f32[48,256]{1,0:T(8,128)}, u32[]{:S(2)}) copy-start(f32[48,256]{1,0:T(8,128)} %param.14) | copy-start | bytes 147460
  328.2 4.0 %copy-start.6 = (f32[48,768]{1,0:T(8,128)S(1)}, f32[48,768]{1,0:T(8,128)}, u32[]{:S(2)}) copy-start(f32[48,768]{1,0:T(8,128)} %param.11) | copy-start | bytes 442372
  328.2 5.5 %copy-start.9 = (f32[8,48]{1,0:T(8,128)S(1)}, f32[8,48]{1,0:T(8,128)}, u32[]{:S(2)}) copy-start(f32[8,48]{1,0:T(8,128)} %param.15) | copy-start | bytes 4612
  328.2 5.5 %copy-start.10 = (f32[8,48]{1,0:T(8,128)S(1)}, f32[8,48]{1,0:T(8,128)}, u32[]{:S(2)}) copy-start(f32[8,48]{1,0:T(8,128)} %param.16) | copy-start | bytes 4612
  328.2 5.5 %copy-start.11 = (f32[8,48]{1,0:T(8,128)S(1)}, f32[8,48]{1,0:T(8,128)}, u32[]{:S(2)}) copy-start(f32[8,48]{1,0:T(8,128)} %param.17) | copy-start | bytes 4612
  332.2 2.3 copy-start.4
  332.2 2.3 copy-start.5
Sparse Core Ops, SparseCore 0:
  11.6 142.7 all-reduce.2
  156.8 146.8 all-reduce.4
